TPU v7x, 32 devices: a whole 2x2x4 slice. The times are simulated.
32 devices in a mesh: shell: 4 (over x, core), sky: 8 (over z, y).
Axes of the slice: x: 2, y: 2, z: 4, core: 2. Of those that a mesh axis runs over, the one named last changes fastest.
Arguments:
- coords: int32 [3, 4, 8, 512], P(None, 'shell', 'sky'), may hold values from 0 to 2047, as said below
- weights: bfloat16 [4, 8, 512], P('shell', 'sky'), may hold values from 0.5 to 2
- live: int32 [4, 8], P('shell', 'sky'), may hold values from 128 to 512, as said below
Outputs:
- jackknife: float32 [4, 64, 600], P('shell', 'sky')
Inputs may be any that keep to these rules, and one draw needn't show every extreme that they name: On device (a, b), coords[0] lies in [a * 256, (a+1) * 256), coords[1] in [b * 256, (b+1) * 256), coords[2] in [0, 1024). `live`: live slots are the first ones of a device; some device is full in every draw.
All inputs are finite; a program needn't handle non-finite values.
Results may differ from a plain program's by a relative error of at most 0.0003.
Values sent between devices are 32-bit elements; how exact they have to be, the bound alone decides.
A program may use at most 64 MiB of HBM per device.

v0:
```python
import math
import jax
import jax.numpy as jnp
from jax import lax
from jax.sharding import PartitionSpec as P

PART_DEV = 512
SIDE_CELLS = 256
SPAN_CELLS = 1024
SUBREGIONS = 8
S_BINS = 30
MU_BINS = 20


def padded(block, sides, width):
    for axis, dim in sides:
        count = lax.axis_size(axis)
        forward = [(i, i + 1) for i in range(count - 1)]
        backward = [(target, source) for source, target in forward]
        low = lax.ppermute(
            lax.slice_in_dim(block, block.shape[dim] - width, None, axis=dim), axis, forward
        )
        high = lax.ppermute(lax.slice_in_dim(block, 0, width, axis=dim), axis, backward)
        block = jnp.concatenate([low, block, high], axis=dim)
    return block


def edge_values():
    return [int(4.0 * 10.0 ** (4.0 * level / S_BINS) + 0.5) for level in range(S_BINS + 1)]


def bin_scale(patches):
    edges = edge_values()
    factor = SIDE_CELLS * SIDE_CELLS * SPAN_CELLS / (patches * PART_DEV * PART_DEV)
    values = []
    for level in range(S_BINS):
        volume = 4.0 * math.pi / 3.0 * (edges[level + 1] ** 1.5 - edges[level] ** 1.5) / MU_BINS
        values = values + [factor / volume] * MU_BINS
    return jnp.asarray(values, dtype=jnp.float32)


def pair_block(own_pos, far_pos, far_weight):
    edges = edge_values()
    radial_gap = jnp.minimum(jnp.abs(own_pos[0][:, None] - far_pos[0][None, :]), 255)
    across_gap = jnp.minimum(jnp.abs(own_pos[1][:, None] - far_pos[1][None, :]), 255)
    depth_gap = jnp.minimum(jnp.abs(own_pos[2][:, None] - far_pos[2][None, :]), 255)
    squared = radial_gap * radial_gap + across_gap * across_gap + depth_gap * depth_gap
    radial_sq = radial_gap * radial_gap * (MU_BINS * MU_BINS)
    s_index = jnp.zeros_like(squared)
    for level in range(1, S_BINS):
        s_index = s_index + (squared >= edges[level]).astype(jnp.int32)
    mu_index = jnp.zeros_like(squared)
    for level in range(1, MU_BINS):
        mu_index = mu_index + (radial_sq >= level * level * squared).astype(jnp.int32)
    inside = (squared >= edges[0]) & (squared < edges[S_BINS])
    s_levels = lax.iota(jnp.int32, S_BINS)
    mu_levels = lax.iota(jnp.int32, MU_BINS)
    s_hot = ((s_index[:, :, None] == s_levels[None, None, :]) & inside[:, :, None]).astype(
        jnp.float32
    )
    s_weighted = (s_hot * far_weight[None, :, None]).astype(jnp.bfloat16)
    mu_hot = (mu_index[:, :, None] == mu_levels[None, None, :]).astype(jnp.bfloat16)
    return jnp.einsum("ijs,ijm->ism", s_weighted, mu_hot, preferred_element_type=jnp.float32)


def local(coords, weights, live):
    live_count = live[0, 0]
    parts = coords.shape[3]
    slots = lax.iota(jnp.int32, parts)
    own_weight = jnp.where(slots < live_count, weights[0, 0].astype(jnp.float32), 0.0)
    own_pos = coords.reshape(3, parts)
    packed = jnp.concatenate(
        [coords.astype(jnp.float32), own_weight.reshape(1, 1, 1, parts)], axis=0
    )
    tile_rows = min(256, parts)
    tiles_live = (live_count + tile_rows - 1) // tile_rows
    empty = jnp.zeros((SUBREGIONS, S_BINS, MU_BINS), jnp.float32)
    region_levels = lax.iota(jnp.int32, SUBREGIONS)
    result = padded(packed, (("shell", 1), ("sky", 2)), 1)
    far_pos = result[:3].reshape(3, 9 * parts).astype(jnp.int32)
    far_weight = result[3].reshape(9 * parts)
    blocks = far_pos.shape[1] // parts

    def add_tile(index, running):
        start = index * tile_rows
        rows_pos = lax.dynamic_slice_in_dim(own_pos, start, tile_rows, 1)
        rows_weight = lax.dynamic_slice_in_dim(own_weight, start, tile_rows, 0)

        def add_block(block, per_row):
            offset = block * parts
            block_pos = lax.dynamic_slice_in_dim(far_pos, offset, parts, 1)
            block_weight = lax.dynamic_slice_in_dim(far_weight, offset, parts, 0)
            return per_row + pair_block(rows_pos, block_pos, block_weight)

        per_row = lax.fori_loop(
            0, blocks, add_block, jnp.zeros((tile_rows, S_BINS, MU_BINS), jnp.float32)
        )
        region = rows_pos[2] // (SPAN_CELLS // SUBREGIONS)
        region_weight = jnp.where(
            region[:, None] == region_levels[None, :], rows_weight[:, None], 0.0
        )
        folded = jnp.sum(region_weight[:, :, None, None] * per_row[:, None, :, :], axis=0)
        return running + folded

    histogram = lax.fori_loop(0, tiles_live, add_tile, empty)
    by_region = histogram.reshape(SUBREGIONS, S_BINS * MU_BINS)
    shell_total = lax.psum(jnp.sum(by_region, axis=0), "sky")
    scale = bin_scale(lax.axis_size("sky"))
    leave = (shell_total[None, :] - by_region) * scale[None, :]
    return leave.reshape(1, SUBREGIONS, S_BINS * MU_BINS)


def solution(mesh):
    in_specs = (P(None, "shell", "sky", None), P("shell", "sky", None), P("shell", "sky"))
    out_specs = P("shell", "sky", None)
    return jax.shard_map(local, mesh=mesh, in_specs=in_specs, out_specs=out_specs, check_vma=False)
```

profile of v0, /device:TPU:2, one launch (start us, length us, event | category | flops | bytes accessed | tf_op | source)
XLA Modules:
  0.0 244.2 jit_solution(1972182534379924726)
XLA Ops:
  0.7 0.7 convert_element_type.570
  2.1 1.9 collective-permute-start.1
  4.0 2.4 collective-permute-start
  6.4 0.7 convert_element_type.575
  7.1 1.9 collective-permute-done
  9.0 1.3 collective-permute-start.3
  10.3 4.5 %collective-permute-start.2 = (f32[4,3,1,512]{3,2,1,0:T(1,128)S(1)}, f32[4,3,1,512]{3,2,1,0:T(1,128)S(1)}, u32[]{:S(2)}, u32[]{:S(2)}) collective-permute-start(f32[4,3,1,512]{3,2,1,0:T(1,128)S(1)} %pad_maximum_fusion.2), channel_id=1, source_target_pairs={{0,1},{1,2},{2,3},{3,4},{4,5},{5,6},{6,7},{8,9},{9,10},{10,11},{11... | collective-permute-start | bytes 73736 | tf_op jit(solution)/shard_map/ppermute | solution.py:20
  14.9 0.7 copy.19
  15.6 0.8 collective-permute-done.2
  16.6 101.9 %while.36 = (s32[]{:T(128)}, f32[8,30,20]{0,2,1:T(8,128)S(1)}, s32[]{:T(128)}, s32[3,512]{1,0:T(4,128)S(1)}, f32[512]{0:T(512)S(1)}, /*index=5*/s32[3,4608]{1,0:...) while((s32[]{:T(128)}, f32[8,30,20]{0,2,1:T(8,128)S(1)}, ...), condition=%wide.region_4.5_spmd.clone, body=%wide.region_0.4_spmd.clone.sunk | while | flops 199642880 | bytes 5579304 | solution.py:105
  16.6 98.5 %while.37 = (s32[]{:T(128)}, f32[256,30,20]{1,2,0:T(8,128)}, s32[3,256]{1,0:T(4,128)S(1)}, s32[3,4608]{1,0:T(4,128)S(1)}, bf16[4608]{0:T(1024)(128)(2,1)S(1)}, /...) while((s32[]{:T(128)}, f32[256,30,20]{1,2,0:T(8,128)}, ...), condition=%wide.region_2.2_spmd.clone, body=%wide.region_1.1_spmd.clone.sunk | while | flops 197177344 | bytes 3628245 | solution.py:95
  16.8 3.3 %convert_add_fusion.3 = (s32[256,512]{1,0:T(8,128)S(1)}, s32[256,512]{1,0:T(8,128)S(1)}) fusion(s32[512]{0:T(512)S(1)} %bitcast.35, s32[256]{0:T(256)S(1)} %bitcast.39, s32[512]{0:T(512)S(1)} %bitcast.31, s32[256]{0:T(256)S(1)} %bitcast.37, s32[512]{0:T(512)S(1)} %bitcast.33, s32[256]{0:T(256)S(1)} %bitcast.41), kind=kLoop, calls=%fused_computation.31.clone.1 | loop fusion | flops 22937600 | bytes 1057792 | tf_op jit(solution)/shard_map/while/body/while/body/eval_jaxpr/add | solution.py:51
  20.7 5.7 %select_add_fusion.2 = f32[256,30,20]{1,2,0:T(8,128)} fusion(f32[256,30,20]{1,2,0:T(8,128)} %get-tuple-element.400, s32[256,512]{1,0:T(8,128)S(1)} %get-tuple-element.386, bf16[512]{0:T(512)(128)(2,1)S(1)} %dynamic_slice.36, s32[256,512]{1,0:T(8,128)S(1)} %get-tuple-element.387, pred[256,512]{1,0:T(8,128)(4,1)S(1)} %compare_and_fusion.2, ...), kind=kOutput, calls=%fused_computation.11.clone.1 | convolution fusion | flops 172011520 | bytes 2409473 | tf_op jit(solution)/shard_map/while/body/while/body/eval_jaxpr/ijs,ijm->ism/dot_general | solution.py:63
  26.5 3.3 %convert_add_fusion.3 = (s32[256,512]{1,0:T(8,128)S(1)}, s32[256,512]{1,0:T(8,128)S(1)}) fusion(s32[512]{0:T(512)S(1)} %bitcast.35, s32[256]{0:T(256)S(1)} %bitcast.39, s32[512]{0:T(512)S(1)} %bitcast.31, s32[256]{0:T(256)S(1)} %bitcast.37, s32[512]{0:T(512)S(1)} %bitcast.33, s32[256]{0:T(256)S(1)} %bitcast.41), kind=kLoop, calls=%fused_computation.31.clone.1 | loop fusion | flops 22937600 | bytes 1057792 | tf_op jit(solution)/shard_map/while/body/while/body/eval_jaxpr/add | solution.py:51
  30.4 7.1 %select_add_fusion.2 = f32[256,30,20]{1,2,0:T(8,128)} fusion(f32[256,30,20]{1,2,0:T(8,128)} %get-tuple-element.400, s32[256,512]{1,0:T(8,128)S(1)} %get-tuple-element.386, bf16[512]{0:T(512)(128)(2,1)S(1)} %dynamic_slice.36, s32[256,512]{1,0:T(8,128)S(1)} %get-tuple-element.387, pred[256,512]{1,0:T(8,128)(4,1)S(1)} %compare_and_fusion.2, ...), kind=kOutput, calls=%fused_computation.11.clone.1 | convolution fusion | flops 172011520 | bytes 2409473 | tf_op jit(solution)/shard_map/while/body/while/body/eval_jaxpr/ijs,ijm->ism/dot_general | solution.py:63
  37.6 3.3 %convert_add_fusion.3 = (s32[256,512]{1,0:T(8,128)S(1)}, s32[256,512]{1,0:T(8,128)S(1)}) fusion(s32[512]{0:T(512)S(1)} %bitcast.35, s32[256]{0:T(256)S(1)} %bitcast.39, s32[512]{0:T(512)S(1)} %bitcast.31, s32[256]{0:T(256)S(1)} %bitcast.37, s32[512]{0:T(512)S(1)} %bitcast.33, s32[256]{0:T(256)S(1)} %bitcast.41), kind=kLoop, calls=%fused_computation.31.clone.1 | loop fusion | flops 22937600 | bytes 1057792 | tf_op jit(solution)/shard_map/while/body/while/body/eval_jaxpr/add | solution.py:51
  41.5 7.1 %select_add_fusion.2 = f32[256,30,20]{1,2,0:T(8,128)} fusion(f32[256,30,20]{1,2,0:T(8,128)} %get-tuple-element.400, s32[256,512]{1,0:T(8,128)S(1)} %get-tuple-element.386, bf16[512]{0:T(512)(128)(2,1)S(1)} %dynamic_slice.36, s32[256,512]{1,0:T(8,128)S(1)} %get-tuple-element.387, pred[256,512]{1,0:T(8,128)(4,1)S(1)} %compare_and_fusion.2, ...), kind=kOutput, calls=%fused_computation.11.clone.1 | convolution fusion | flops 172011520 | bytes 2409473 | tf_op jit(solution)/shard_map/while/body/while/body/eval_jaxpr/ijs,ijm->ism/dot_general | solution.py:63
  48.7 3.3 %convert_add_fusion.3 = (s32[256,512]{1,0:T(8,128)S(1)}, s32[256,512]{1,0:T(8,128)S(1)}) fusion(s32[512]{0:T(512)S(1)} %bitcast.35, s32[256]{0:T(256)S(1)} %bitcast.39, s32[512]{0:T(512)S(1)} %bitcast.31, s32[256]{0:T(256)S(1)} %bitcast.37, s32[512]{0:T(512)S(1)} %bitcast.33, s32[256]{0:T(256)S(1)} %bitcast.41), kind=kLoop, calls=%fused_computation.31.clone.1 | loop fusion | flops 22937600 | bytes 1057792 | tf_op jit(solution)/shard_map/while/body/while/body/eval_jaxpr/add | solution.py:51
  52.6 7.1 %select_add_fusion.2 = f32[256,30,20]{1,2,0:T(8,128)} fusion(f32[256,30,20]{1,2,0:T(8,128)} %get-tuple-element.400, s32[256,512]{1,0:T(8,128)S(1)} %get-tuple-element.386, bf16[512]{0:T(512)(128)(2,1)S(1)} %dynamic_slice.36, s32[256,512]{1,0:T(8,128)S(1)} %get-tuple-element.387, pred[256,512]{1,0:T(8,128)(4,1)S(1)} %compare_and_fusion.2, ...), kind=kOutput, calls=%fused_computation.11.clone.1 | convolution fusion | flops 172011520 | bytes 2409473 | tf_op jit(solution)/shard_map/while/body/while/body/eval_jaxpr/ijs,ijm->ism/dot_general | solution.py:63
  59.8 3.3 %convert_add_fusion.3 = (s32[256,512]{1,0:T(8,128)S(1)}, s32[256,512]{1,0:T(8,128)S(1)}) fusion(s32[512]{0:T(512)S(1)} %bitcast.35, s32[256]{0:T(256)S(1)} %bitcast.39, s32[512]{0:T(512)S(1)} %bitcast.31, s32[256]{0:T(256)S(1)} %bitcast.37, s32[512]{0:T(512)S(1)} %bitcast.33, s32[256]{0:T(256)S(1)} %bitcast.41), kind=kLoop, calls=%fused_computation.31.clone.1 | loop fusion | flops 22937600 | bytes 1057792 | tf_op jit(solution)/shard_map/while/body/while/body/eval_jaxpr/add | solution.py:51
  63.7 7.1 %select_add_fusion.2 = f32[256,30,20]{1,2,0:T(8,128)} fusion(f32[256,30,20]{1,2,0:T(8,128)} %get-tuple-element.400, s32[256,512]{1,0:T(8,128)S(1)} %get-tuple-element.386, bf16[512]{0:T(512)(128)(2,1)S(1)} %dynamic_slice.36, s32[256,512]{1,0:T(8,128)S(1)} %get-tuple-element.387, pred[256,512]{1,0:T(8,128)(4,1)S(1)} %compare_and_fusion.2, ...), kind=kOutput, calls=%fused_computation.11.clone.1 | convolution fusion | flops 172011520 | bytes 2409473 | tf_op jit(solution)/shard_map/while/body/while/body/eval_jaxpr/ijs,ijm->ism/dot_general | solution.py:63
  70.8 3.3 %convert_add_fusion.3 = (s32[256,512]{1,0:T(8,128)S(1)}, s32[256,512]{1,0:T(8,128)S(1)}) fusion(s32[512]{0:T(512)S(1)} %bitcast.35, s32[256]{0:T(256)S(1)} %bitcast.39, s32[512]{0:T(512)S(1)} %bitcast.31, s32[256]{0:T(256)S(1)} %bitcast.37, s32[512]{0:T(512)S(1)} %bitcast.33, s32[256]{0:T(256)S(1)} %bitcast.41), kind=kLoop, calls=%fused_computation.31.clone.1 | loop fusion | flops 22937600 | bytes 1057792 | tf_op jit(solution)/shard_map/while/body/while/body/eval_jaxpr/add | solution.py:51
  74.8 7.1 %select_add_fusion.2 = f32[256,30,20]{1,2,0:T(8,128)} fusion(f32[256,30,20]{1,2,0:T(8,128)} %get-tuple-element.400, s32[256,512]{1,0:T(8,128)S(1)} %get-tuple-element.386, bf16[512]{0:T(512)(128)(2,1)S(1)} %dynamic_slice.36, s32[256,512]{1,0:T(8,128)S(1)} %get-tuple-element.387, pred[256,512]{1,0:T(8,128)(4,1)S(1)} %compare_and_fusion.2, ...), kind=kOutput, calls=%fused_computation.11.clone.1 | convolution fusion | flops 172011520 | bytes 2409473 | tf_op jit(solution)/shard_map/while/body/while/body/eval_jaxpr/ijs,ijm->ism/dot_general | solution.py:63
  81.9 3.3 %convert_add_fusion.3 = (s32[256,512]{1,0:T(8,128)S(1)}, s32[256,512]{1,0:T(8,128)S(1)}) fusion(s32[512]{0:T(512)S(1)} %bitcast.35, s32[256]{0:T(256)S(1)} %bitcast.39, s32[512]{0:T(512)S(1)} %bitcast.31, s32[256]{0:T(256)S(1)} %bitcast.37, s32[512]{0:T(512)S(1)} %bitcast.33, s32[256]{0:T(256)S(1)} %bitcast.41), kind=kLoop, calls=%fused_computation.31.clone.1 | loop fusion | flops 22937600 | bytes 1057792 | tf_op jit(solution)/shard_map/while/body/while/body/eval_jaxpr/add | solution.py:51
  85.9 7.1 %select_add_fusion.2 = f32[256,30,20]{1,2,0:T(8,128)} fusion(f32[256,30,20]{1,2,0:T(8,128)} %get-tuple-element.400, s32[256,512]{1,0:T(8,128)S(1)} %get-tuple-element.386, bf16[512]{0:T(512)(128)(2,1)S(1)} %dynamic_slice.36, s32[256,512]{1,0:T(8,128)S(1)} %get-tuple-element.387, pred[256,512]{1,0:T(8,128)(4,1)S(1)} %compare_and_fusion.2, ...), kind=kOutput, calls=%fused_computation.11.clone.1 | convolution fusion | flops 172011520 | bytes 2409473 | tf_op jit(solution)/shard_map/while/body/while/body/eval_jaxpr/ijs,ijm->ism/dot_general | solution.py:63
  93.0 3.3 %convert_add_fusion.3 = (s32[256,512]{1,0:T(8,128)S(1)}, s32[256,512]{1,0:T(8,128)S(1)}) fusion(s32[512]{0:T(512)S(1)} %bitcast.35, s32[256]{0:T(256)S(1)} %bitcast.39, s32[512]{0:T(512)S(1)} %bitcast.31, s32[256]{0:T(256)S(1)} %bitcast.37, s32[512]{0:T(512)S(1)} %bitcast.33, s32[256]{0:T(256)S(1)} %bitcast.41), kind=kLoop, calls=%fused_computation.31.clone.1 | loop fusion | flops 22937600 | bytes 1057792 | tf_op jit(solution)/shard_map/while/body/while/body/eval_jaxpr/add | solution.py:51
  96.9 7.1 %select_add_fusion.2 = f32[256,30,20]{1,2,0:T(8,128)} fusion(f32[256,30,20]{1,2,0:T(8,128)} %get-tuple-element.400, s32[256,512]{1,0:T(8,128)S(1)} %get-tuple-element.386, bf16[512]{0:T(512)(128)(2,1)S(1)} %dynamic_slice.36, s32[256,512]{1,0:T(8,128)S(1)} %get-tuple-element.387, pred[256,512]{1,0:T(8,128)(4,1)S(1)} %compare_and_fusion.2, ...), kind=kOutput, calls=%fused_computation.11.clone.1 | convolution fusion | flops 172011520 | bytes 2409473 | tf_op jit(solution)/shard_map/while/body/while/body/eval_jaxpr/ijs,ijm->ism/dot_general | solution.py:63
  104.1 3.3 %convert_add_fusion.3 = (s32[256,512]{1,0:T(8,128)S(1)}, s32[256,512]{1,0:T(8,128)S(1)}) fusion(s32[512]{0:T(512)S(1)} %bitcast.35, s32[256]{0:T(256)S(1)} %bitcast.39, s32[512]{0:T(512)S(1)} %bitcast.31, s32[256]{0:T(256)S(1)} %bitcast.37, s32[512]{0:T(512)S(1)} %bitcast.33, s32[256]{0:T(256)S(1)} %bitcast.41), kind=kLoop, calls=%fused_computation.31.clone.1 | loop fusion | flops 22937600 | bytes 1057792 | tf_op jit(solution)/shard_map/while/body/while/body/eval_jaxpr/add | solution.py:51
  108.0 7.1 %select_add_fusion.2 = f32[256,30,20]{1,2,0:T(8,128)} fusion(f32[256,30,20]{1,2,0:T(8,128)} %get-tuple-element.400, s32[256,512]{1,0:T(8,128)S(1)} %get-tuple-element.386, bf16[512]{0:T(512)(128)(2,1)S(1)} %dynamic_slice.36, s32[256,512]{1,0:T(8,128)S(1)} %get-tuple-element.387, pred[256,512]{1,0:T(8,128)(4,1)S(1)} %compare_and_fusion.2, ...), kind=kOutput, calls=%fused_computation.11.clone.1 | convolution fusion | flops 172011520 | bytes 2409473 | tf_op jit(solution)/shard_map/while/body/while/body/eval_jaxpr/ijs,ijm->ism/dot_general | solution.py:63
  115.1 2.4 copy.21
  117.7 0.7 multiply_reduce_fusion.2
  119.2 124.4 %psum.7 = f32[600]{0:T(1024)S(1)} all-reduce(f32[600]{0:T(1024)S(1)} %reduce_sum.24), channel_id=1, replica_groups=mesh['shell'=4,'sky'=8] {'sky'}, use_global_device_ids=true, to_apply=%region_6.7 | all-reduce | flops 600 | bytes 4800 | tf_op jit(solution)/shard_map/psum | solution.py:107
  (62 shorter events, 9.0 us)
Async XLA Ops:
  2.1 5.0 %collective-permute-start.1 = (f32[4,1,1,512]{3,2,1,0:T(1,128)S(1)}, f32[4,1,1,512]{3,2,1,0:T(1,128)S(1)}, u32[]{:S(2)}, u32[]{:S(2)}) collective-permute-start(f32[4,1,1,512]{3,2,1,0:T(1,128)S(1)} %pad_maximum_fusion.3), channel_id=1, source_target_pairs={{8,0},{16,8},{24,16},{9,1},{17,9},{25,17},{10,2},{18,10},{26,18},{... | collective-permute-start | bytes 24584 | tf_op jit(solution)/shard_map/ppermute | solution.py:23
  4.0 5.0 %collective-permute-start = (f32[4,1,1,512]{3,2,1,0:T(1,128)S(1)}, f32[4,1,1,512]{3,2,1,0:T(1,128)S(1)}, u32[]{:S(2)}, u32[]{:S(2)}) collective-permute-start(f32[4,1,1,512]{3,2,1,0:T(1,128)S(1)} %pad_maximum_fusion.3), channel_id=1, source_target_pairs={{0,8},{8,16},{16,24},{1,9},{9,17},{17,25},{2,10},{10,18},{18,26},{... | collective-permute-start | bytes 24584 | tf_op jit(solution)/shard_map/ppermute | solution.py:20
  9.0 6.6 %collective-permute-start.3 = (f32[4,3,1,512]{3,2,1,0:T(1,128)S(1)}, f32[4,3,1,512]{3,2,1,0:T(1,128)S(1)}, u32[]{:S(2)}, u32[]{:S(2)}) collective-permute-start(f32[4,3,1,512]{3,2,1,0:T(1,128)S(1)} %pad_maximum_fusion.2), channel_id=1, source_target_pairs={{1,0},{2,1},{3,2},{4,3},{5,4},{6,5},{7,6},{9,8},{10,9},{11,10},{12... | collective-permute-start | bytes 73736 | tf_op jit(solution)/shard_map/ppermute | solution.py:23
  10.3 6.1 %collective-permute-start.2 = (f32[4,3,1,512]{3,2,1,0:T(1,128)S(1)}, f32[4,3,1,512]{3,2,1,0:T(1,128)S(1)}, u32[]{:S(2)}, u32[]{:S(2)}) collective-permute-start(f32[4,3,1,512]{3,2,1,0:T(1,128)S(1)} %pad_maximum_fusion.2), channel_id=1, source_target_pairs={{0,1},{1,2},{2,3},{3,4},{4,5},{5,6},{6,7},{8,9},{9,10},{10,11},{11... | collective-permute-start | bytes 73736 | tf_op jit(solution)/shard_map/ppermute | solution.py:20
  16.6 227.0 %copy-start = (f32[600]{0:T(1024)S(1)}, f32[600]{0:T(1024)}, u32[]{:S(2)}) copy-start(f32[600]{0:T(1024)} %constant.397.clone) | copy-start | bytes 7204
where the time goes:
time: 245 us; the launch traced here: 244 us
  blocking collectives  124 us (51%)
  matrix products  62.4 us (25%)
  other arithmetic  38.2 us (16%)
  starting transfers between devices  10.2 us (4%)
  local copies, waits for them, and re-layouts  5.34 us (2%)
  waiting for transfers between devices  2.65 us (1%)
    psum x1, blocking collectives, local(): shell_total = lax.psum(jnp.sum(by_region, axis=0), 'sky')  124 us
    dot_general x9, matrix products, pair_block(): jnp.einsum('ijs,ijm->ism', s_weighted, mu_hot, preferred_element_type=jnp...  62.4 us
    add x9, other arithmetic, pair_block(): s_index = s_index + (squared >= edges[level]).astype(jnp.int32)  29.3 us
    ppermute x2, starting transfers between devices, padded(): lax.ppermute(lax.slice_in_dim(block, block.shape[dim] - width, None, axis...  6.95 us
    and x9, other arithmetic, pair_block(): inside = (squared >= edges[0]) & (squared < edges[S_BINS])  5.04 us
  transfers between devices with their start and end apart: 4, of which 2 were waited for; matrix products, arithmetic and copies ran while one was open for 1% of the time, Pallas kernels for 0%

commit v1 on v0

--- a/solution.py
+++ b/solution.py
@@ -104,7 +104,7 @@
 
     histogram = lax.fori_loop(0, tiles_live, add_tile, empty)
     by_region = histogram.reshape(SUBREGIONS, S_BINS * MU_BINS)
-    shell_total = lax.psum(jnp.sum(by_region, axis=0), "sky")
+    shell_total = jnp.sum(lax.all_gather(jnp.sum(by_region, axis=0), "sky"), axis=0)
     scale = bin_scale(lax.axis_size("sky"))
     leave = (shell_total[None, :] - by_region) * scale[None, :]
     return leave.reshape(1, SUBREGIONS, S_BINS * MU_BINS)

time: 245 us -> 254 us (1.037)
  blocking collectives: 124 us -> 133 us
    all_gather x0 -> x1, blocking collectives: none -> 133 us  [local(): lax.all_gather(jnp.sum(by_region, axis=0), 'sky')]
    psum x1 -> x0, blocking collectives: 124 us -> none  [local(): shell_total = lax.psum(jnp.sum(by_region, axis=0), 'sky')]
where the time goes in v1:
time: 254 us; the launch traced here: 253 us
  blocking collectives  133 us (52%)
  matrix products  62.4 us (25%)
  other arithmetic  38.2 us (15%)
  starting transfers between devices  10.2 us (4%)
  local copies, waits for them, and re-layouts  5.35 us (2%)
  waiting for transfers between devices  2.65 us (1%)
    all_gather x1, blocking collectives, local(): lax.all_gather(jnp.sum(by_region, axis=0), 'sky')  133 us
    dot_general x9, matrix products, pair_block(): jnp.einsum('ijs,ijm->ism', s_weighted, mu_hot, preferred_element_type=jnp...  62.4 us
    add x9, other arithmetic, pair_block(): s_index = s_index + (squared >= edges[level]).astype(jnp.int32)  29.3 us
    ppermute x2, starting transfers between devices, padded(): lax.ppermute(lax.slice_in_dim(block, block.shape[dim] - width, None, axis...  6.95 us
  transfers between devices with their start and end apart: 4, of which 2 were waited for; matrix products, arithmetic and copies ran while one was open for 1% of the time, Pallas kernels for 0%

profile of v1, /device:TPU:2, one launch (start us, length us, event | category | flops | bytes accessed | tf_op | source)
XLA Modules:
  0.0 252.8 jit_solution(6490611206848121961)
XLA Ops:
  0.7 0.7 convert_element_type.570
  2.1 1.9 collective-permute-start.1
  4.0 2.4 collective-permute-start
  6.4 0.7 convert_element_type.575
  7.1 1.9 collective-permute-done
  9.0 1.3 collective-permute-start.3
  10.3 4.5 %collective-permute-start.2 = (f32[4,3,1,512]{3,2,1,0:T(1,128)S(1)}, f32[4,3,1,512]{3,2,1,0:T(1,128)S(1)}, u32[]{:S(2)}, u32[]{:S(2)}) collective-permute-start(f32[4,3,1,512]{3,2,1,0:T(1,128)S(1)} %pad_maximum_fusion.2), channel_id=1, source_target_pairs={{0,1},{1,2},{2,3},{3,4},{4,5},{5,6},{6,7},{8,9},{9,10},{10,11},{11... | collective-permute-start | bytes 73736 | tf_op jit(solution)/shard_map/ppermute | solution.py:20
  14.9 0.7 copy.19
  15.6 0.8 collective-permute-done.2
  16.6 101.9 %while.36 = (s32[]{:T(128)}, f32[8,30,20]{0,2,1:T(8,128)S(1)}, s32[]{:T(128)}, s32[3,512]{1,0:T(4,128)S(1)}, f32[512]{0:T(512)S(1)}, /*index=5*/s32[3,4608]{1,0:...) while((s32[]{:T(128)}, f32[8,30,20]{0,2,1:T(8,128)S(1)}, ...), condition=%wide.region_4.5_spmd.clone, body=%wide.region_0.4_spmd.clone.sunk | while | flops 199642880 | bytes 5579304 | solution.py:105
  16.6 98.5 %while.37 = (s32[]{:T(128)}, f32[256,30,20]{1,2,0:T(8,128)}, s32[3,256]{1,0:T(4,128)S(1)}, s32[3,4608]{1,0:T(4,128)S(1)}, bf16[4608]{0:T(1024)(128)(2,1)S(1)}, /...) while((s32[]{:T(128)}, f32[256,30,20]{1,2,0:T(8,128)}, ...), condition=%wide.region_2.2_spmd.clone, body=%wide.region_1.1_spmd.clone.sunk | while | flops 197177344 | bytes 3628245 | solution.py:95
  16.8 3.3 %convert_add_fusion.3 = (s32[256,512]{1,0:T(8,128)S(1)}, s32[256,512]{1,0:T(8,128)S(1)}) fusion(s32[512]{0:T(512)S(1)} %bitcast.35, s32[256]{0:T(256)S(1)} %bitcast.39, s32[512]{0:T(512)S(1)} %bitcast.31, s32[256]{0:T(256)S(1)} %bitcast.37, s32[512]{0:T(512)S(1)} %bitcast.33, s32[256]{0:T(256)S(1)} %bitcast.41), kind=kLoop, calls=%fused_computation.31.clone.1 | loop fusion | flops 22937600 | bytes 1057792 | tf_op jit(solution)/shard_map/while/body/while/body/eval_jaxpr/add | solution.py:51
  20.7 5.7 %select_add_fusion.2 = f32[256,30,20]{1,2,0:T(8,128)} fusion(f32[256,30,20]{1,2,0:T(8,128)} %get-tuple-element.400, s32[256,512]{1,0:T(8,128)S(1)} %get-tuple-element.386, bf16[512]{0:T(512)(128)(2,1)S(1)} %dynamic_slice.36, s32[256,512]{1,0:T(8,128)S(1)} %get-tuple-element.387, pred[256,512]{1,0:T(8,128)(4,1)S(1)} %compare_and_fusion.2, ...), kind=kOutput, calls=%fused_computation.11.clone.1 | convolution fusion | flops 172011520 | bytes 2409473 | tf_op jit(solution)/shard_map/while/body/while/body/eval_jaxpr/ijs,ijm->ism/dot_general | solution.py:63
  26.5 3.3 %convert_add_fusion.3 = (s32[256,512]{1,0:T(8,128)S(1)}, s32[256,512]{1,0:T(8,128)S(1)}) fusion(s32[512]{0:T(512)S(1)} %bitcast.35, s32[256]{0:T(256)S(1)} %bitcast.39, s32[512]{0:T(512)S(1)} %bitcast.31, s32[256]{0:T(256)S(1)} %bitcast.37, s32[512]{0:T(512)S(1)} %bitcast.33, s32[256]{0:T(256)S(1)} %bitcast.41), kind=kLoop, calls=%fused_computation.31.clone.1 | loop fusion | flops 22937600 | bytes 1057792 | tf_op jit(solution)/shard_map/while/body/while/body/eval_jaxpr/add | solution.py:51
  30.4 7.1 %select_add_fusion.2 = f32[256,30,20]{1,2,0:T(8,128)} fusion(f32[256,30,20]{1,2,0:T(8,128)} %get-tuple-element.400, s32[256,512]{1,0:T(8,128)S(1)} %get-tuple-element.386, bf16[512]{0:T(512)(128)(2,1)S(1)} %dynamic_slice.36, s32[256,512]{1,0:T(8,128)S(1)} %get-tuple-element.387, pred[256,512]{1,0:T(8,128)(4,1)S(1)} %compare_and_fusion.2, ...), kind=kOutput, calls=%fused_computation.11.clone.1 | convolution fusion | flops 172011520 | bytes 2409473 | tf_op jit(solution)/shard_map/while/body/while/body/eval_jaxpr/ijs,ijm->ism/dot_general | solution.py:63
  37.6 3.3 %convert_add_fusion.3 = (s32[256,512]{1,0:T(8,128)S(1)}, s32[256,512]{1,0:T(8,128)S(1)}) fusion(s32[512]{0:T(512)S(1)} %bitcast.35, s32[256]{0:T(256)S(1)} %bitcast.39, s32[512]{0:T(512)S(1)} %bitcast.31, s32[256]{0:T(256)S(1)} %bitcast.37, s32[512]{0:T(512)S(1)} %bitcast.33, s32[256]{0:T(256)S(1)} %bitcast.41), kind=kLoop, calls=%fused_computation.31.clone.1 | loop fusion | flops 22937600 | bytes 1057792 | tf_op jit(solution)/shard_map/while/body/while/body/eval_jaxpr/add | solution.py:51
  41.5 7.1 %select_add_fusion.2 = f32[256,30,20]{1,2,0:T(8,128)} fusion(f32[256,30,20]{1,2,0:T(8,128)} %get-tuple-element.400, s32[256,512]{1,0:T(8,128)S(1)} %get-tuple-element.386, bf16[512]{0:T(512)(128)(2,1)S(1)} %dynamic_slice.36, s32[256,512]{1,0:T(8,128)S(1)} %get-tuple-element.387, pred[256,512]{1,0:T(8,128)(4,1)S(1)} %compare_and_fusion.2, ...), kind=kOutput, calls=%fused_computation.11.clone.1 | convolution fusion | flops 172011520 | bytes 2409473 | tf_op jit(solution)/shard_map/while/body/while/body/eval_jaxpr/ijs,ijm->ism/dot_general | solution.py:63
  48.7 3.3 %convert_add_fusion.3 = (s32[256,512]{1,0:T(8,128)S(1)}, s32[256,512]{1,0:T(8,128)S(1)}) fusion(s32[512]{0:T(512)S(1)} %bitcast.35, s32[256]{0:T(256)S(1)} %bitcast.39, s32[512]{0:T(512)S(1)} %bitcast.31, s32[256]{0:T(256)S(1)} %bitcast.37, s32[512]{0:T(512)S(1)} %bitcast.33, s32[256]{0:T(256)S(1)} %bitcast.41), kind=kLoop, calls=%fused_computation.31.clone.1 | loop fusion | flops 22937600 | bytes 1057792 | tf_op jit(solution)/shard_map/while/body/while/body/eval_jaxpr/add | solution.py:51
  52.6 7.1 %select_add_fusion.2 = f32[256,30,20]{1,2,0:T(8,128)} fusion(f32[256,30,20]{1,2,0:T(8,128)} %get-tuple-element.400, s32[256,512]{1,0:T(8,128)S(1)} %get-tuple-element.386, bf16[512]{0:T(512)(128)(2,1)S(1)} %dynamic_slice.36, s32[256,512]{1,0:T(8,128)S(1)} %get-tuple-element.387, pred[256,512]{1,0:T(8,128)(4,1)S(1)} %compare_and_fusion.2, ...), kind=kOutput, calls=%fused_computation.11.clone.1 | convolution fusion | flops 172011520 | bytes 2409473 | tf_op jit(solution)/shard_map/while/body/while/body/eval_jaxpr/ijs,ijm->ism/dot_general | solution.py:63
  59.8 3.3 %convert_add_fusion.3 = (s32[256,512]{1,0:T(8,128)S(1)}, s32[256,512]{1,0:T(8,128)S(1)}) fusion(s32[512]{0:T(512)S(1)} %bitcast.35, s32[256]{0:T(256)S(1)} %bitcast.39, s32[512]{0:T(512)S(1)} %bitcast.31, s32[256]{0:T(256)S(1)} %bitcast.37, s32[512]{0:T(512)S(1)} %bitcast.33, s32[256]{0:T(256)S(1)} %bitcast.41), kind=kLoop, calls=%fused_computation.31.clone.1 | loop fusion | flops 22937600 | bytes 1057792 | tf_op jit(solution)/shard_map/while/body/while/body/eval_jaxpr/add | solution.py:51
  63.7 7.1 %select_add_fusion.2 = f32[256,30,20]{1,2,0:T(8,128)} fusion(f32[256,30,20]{1,2,0:T(8,128)} %get-tuple-element.400, s32[256,512]{1,0:T(8,128)S(1)} %get-tuple-element.386, bf16[512]{0:T(512)(128)(2,1)S(1)} %dynamic_slice.36, s32[256,512]{1,0:T(8,128)S(1)} %get-tuple-element.387, pred[256,512]{1,0:T(8,128)(4,1)S(1)} %compare_and_fusion.2, ...), kind=kOutput, calls=%fused_computation.11.clone.1 | convolution fusion | flops 172011520 | bytes 2409473 | tf_op jit(solution)/shard_map/while/body/while/body/eval_jaxpr/ijs,ijm->ism/dot_general | solution.py:63
  70.8 3.3 %convert_add_fusion.3 = (s32[256,512]{1,0:T(8,128)S(1)}, s32[256,512]{1,0:T(8,128)S(1)}) fusion(s32[512]{0:T(512)S(1)} %bitcast.35, s32[256]{0:T(256)S(1)} %bitcast.39, s32[512]{0:T(512)S(1)} %bitcast.31, s32[256]{0:T(256)S(1)} %bitcast.37, s32[512]{0:T(512)S(1)} %bitcast.33, s32[256]{0:T(256)S(1)} %bitcast.41), kind=kLoop, calls=%fused_computation.31.clone.1 | loop fusion | flops 22937600 | bytes 1057792 | tf_op jit(solution)/shard_map/while/body/while/body/eval_jaxpr/add | solution.py:51
  74.8 7.1 %select_add_fusion.2 = f32[256,30,20]{1,2,0:T(8,128)} fusion(f32[256,30,20]{1,2,0:T(8,128)} %get-tuple-element.400, s32[256,512]{1,0:T(8,128)S(1)} %get-tuple-element.386, bf16[512]{0:T(512)(128)(2,1)S(1)} %dynamic_slice.36, s32[256,512]{1,0:T(8,128)S(1)} %get-tuple-element.387, pred[256,512]{1,0:T(8,128)(4,1)S(1)} %compare_and_fusion.2, ...), kind=kOutput, calls=%fused_computation.11.clone.1 | convolution fusion | flops 172011520 | bytes 2409473 | tf_op jit(solution)/shard_map/while/body/while/body/eval_jaxpr/ijs,ijm->ism/dot_general | solution.py:63
  81.9 3.3 %convert_add_fusion.3 = (s32[256,512]{1,0:T(8,128)S(1)}, s32[256,512]{1,0:T(8,128)S(1)}) fusion(s32[512]{0:T(512)S(1)} %bitcast.35, s32[256]{0:T(256)S(1)} %bitcast.39, s32[512]{0:T(512)S(1)} %bitcast.31, s32[256]{0:T(256)S(1)} %bitcast.37, s32[512]{0:T(512)S(1)} %bitcast.33, s32[256]{0:T(256)S(1)} %bitcast.41), kind=kLoop, calls=%fused_computation.31.clone.1 | loop fusion | flops 22937600 | bytes 1057792 | tf_op jit(solution)/shard_map/while/body/while/body/eval_jaxpr/add | solution.py:51
  85.9 7.1 %select_add_fusion.2 = f32[256,30,20]{1,2,0:T(8,128)} fusion(f32[256,30,20]{1,2,0:T(8,128)} %get-tuple-element.400, s32[256,512]{1,0:T(8,128)S(1)} %get-tuple-element.386, bf16[512]{0:T(512)(128)(2,1)S(1)} %dynamic_slice.36, s32[256,512]{1,0:T(8,128)S(1)} %get-tuple-element.387, pred[256,512]{1,0:T(8,128)(4,1)S(1)} %compare_and_fusion.2, ...), kind=kOutput, calls=%fused_computation.11.clone.1 | convolution fusion | flops 172011520 | bytes 2409473 | tf_op jit(solution)/shard_map/while/body/while/body/eval_jaxpr/ijs,ijm->ism/dot_general | solution.py:63
  93.0 3.3 %convert_add_fusion.3 = (s32[256,512]{1,0:T(8,128)S(1)}, s32[256,512]{1,0:T(8,128)S(1)}) fusion(s32[512]{0:T(512)S(1)} %bitcast.35, s32[256]{0:T(256)S(1)} %bitcast.39, s32[512]{0:T(512)S(1)} %bitcast.31, s32[256]{0:T(256)S(1)} %bitcast.37, s32[512]{0:T(512)S(1)} %bitcast.33, s32[256]{0:T(256)S(1)} %bitcast.41), kind=kLoop, calls=%fused_computation.31.clone.1 | loop fusion | flops 22937600 | bytes 1057792 | tf_op jit(solution)/shard_map/while/body/while/body/eval_jaxpr/add | solution.py:51
  96.9 7.1 %select_add_fusion.2 = f32[256,30,20]{1,2,0:T(8,128)} fusion(f32[256,30,20]{1,2,0:T(8,128)} %get-tuple-element.400, s32[256,512]{1,0:T(8,128)S(1)} %get-tuple-element.386, bf16[512]{0:T(512)(128)(2,1)S(1)} %dynamic_slice.36, s32[256,512]{1,0:T(8,128)S(1)} %get-tuple-element.387, pred[256,512]{1,0:T(8,128)(4,1)S(1)} %compare_and_fusion.2, ...), kind=kOutput, calls=%fused_computation.11.clone.1 | convolution fusion | flops 172011520 | bytes 2409473 | tf_op jit(solution)/shard_map/while/body/while/body/eval_jaxpr/ijs,ijm->ism/dot_general | solution.py:63
  104.1 3.3 %convert_add_fusion.3 = (s32[256,512]{1,0:T(8,128)S(1)}, s32[256,512]{1,0:T(8,128)S(1)}) fusion(s32[512]{0:T(512)S(1)} %bitcast.35, s32[256]{0:T(256)S(1)} %bitcast.39, s32[512]{0:T(512)S(1)} %bitcast.31, s32[256]{0:T(256)S(1)} %bitcast.37, s32[512]{0:T(512)S(1)} %bitcast.33, s32[256]{0:T(256)S(1)} %bitcast.41), kind=kLoop, calls=%fused_computation.31.clone.1 | loop fusion | flops 22937600 | bytes 1057792 | tf_op jit(solution)/shard_map/while/body/while/body/eval_jaxpr/add | solution.py:51
  108.0 7.1 %select_add_fusion.2 = f32[256,30,20]{1,2,0:T(8,128)} fusion(f32[256,30,20]{1,2,0:T(8,128)} %get-tuple-element.400, s32[256,512]{1,0:T(8,128)S(1)} %get-tuple-element.386, bf16[512]{0:T(512)(128)(2,1)S(1)} %dynamic_slice.36, s32[256,512]{1,0:T(8,128)S(1)} %get-tuple-element.387, pred[256,512]{1,0:T(8,128)(4,1)S(1)} %compare_and_fusion.2, ...), kind=kOutput, calls=%fused_computation.11.clone.1 | convolution fusion | flops 172011520 | bytes 2409473 | tf_op jit(solution)/shard_map/while/body/while/body/eval_jaxpr/ijs,ijm->ism/dot_general | solution.py:63
  115.1 2.4 copy.21
  117.7 0.7 multiply_reduce_fusion.2
  119.2 133.0 %all-gather = f32[8,1,600]{2,1,0:T(1,128)S(1)} all-gather(f32[1,1,600]{2,1,0:T(1,128)S(1)} %reshape.666), channel_id=1, replica_groups=mesh['shell'=4,'sky'=8] {'sky'}, dimensions={0}, use_global_device_ids=true | all-gather | bytes 21600 | tf_op jit(solution)/shard_map/all_gather | solution.py:107
  (63 shorter events, 9.0 us)
Async XLA Ops:
  2.1 5.0 %collective-permute-start.1 = (f32[4,1,1,512]{3,2,1,0:T(1,128)S(1)}, f32[4,1,1,512]{3,2,1,0:T(1,128)S(1)}, u32[]{:S(2)}, u32[]{:S(2)}) collective-permute-start(f32[4,1,1,512]{3,2,1,0:T(1,128)S(1)} %pad_maximum_fusion.3), channel_id=1, source_target_pairs={{8,0},{16,8},{24,16},{9,1},{17,9},{25,17},{10,2},{18,10},{26,18},{... | collective-permute-start | bytes 24584 | tf_op jit(solution)/shard_map/ppermute | solution.py:23
  4.0 5.0 %collective-permute-start = (f32[4,1,1,512]{3,2,1,0:T(1,128)S(1)}, f32[4,1,1,512]{3,2,1,0:T(1,128)S(1)}, u32[]{:S(2)}, u32[]{:S(2)}) collective-permute-start(f32[4,1,1,512]{3,2,1,0:T(1,128)S(1)} %pad_maximum_fusion.3), channel_id=1, source_target_pairs={{0,8},{8,16},{16,24},{1,9},{9,17},{17,25},{2,10},{10,18},{18,26},{... | collective-permute-start | bytes 24584 | tf_op jit(solution)/shard_map/ppermute | solution.py:20
  9.0 6.6 %collective-permute-start.3 = (f32[4,3,1,512]{3,2,1,0:T(1,128)S(1)}, f32[4,3,1,512]{3,2,1,0:T(1,128)S(1)}, u32[]{:S(2)}, u32[]{:S(2)}) collective-permute-start(f32[4,3,1,512]{3,2,1,0:T(1,128)S(1)} %pad_maximum_fusion.2), channel_id=1, source_target_pairs={{1,0},{2,1},{3,2},{4,3},{5,4},{6,5},{7,6},{9,8},{10,9},{11,10},{12... | collective-permute-start | bytes 73736 | tf_op jit(solution)/shard_map/ppermute | solution.py:23
  10.3 6.1 %collective-permute-start.2 = (f32[4,3,1,512]{3,2,1,0:T(1,128)S(1)}, f32[4,3,1,512]{3,2,1,0:T(1,128)S(1)}, u32[]{:S(2)}, u32[]{:S(2)}) collective-permute-start(f32[4,3,1,512]{3,2,1,0:T(1,128)S(1)} %pad_maximum_fusion.2), channel_id=1, source_target_pairs={{0,1},{1,2},{2,3},{3,4},{4,5},{5,6},{6,7},{8,9},{9,10},{10,11},{11... | collective-permute-start | bytes 73736 | tf_op jit(solution)/shard_map/ppermute | solution.py:20
  16.6 235.6 %copy-start = (f32[600]{0:T(1024)S(1)}, f32[600]{0:T(1024)}, u32[]{:S(2)}) copy-start(f32[600]{0:T(1024)} %constant.397.clone) | copy-start | bytes 7204
